TPU v7x, 256 devices: a whole 4x4x8 slice. The times are simulated.
256 devices in a mesh: seg: 8 (over z), src: 32 (over x, y, core).
Axes of the slice: x: 4, y: 4, z: 8, core: 2. Of those that a mesh axis runs over, the one named last changes fastest.
Arguments:
- attitude_partials: bfloat16 [8, 4, 524288], P('seg', None, 'src'), may hold values from -0.59765625 to 0.59765625
- scan_phase: float32 [8, 524288], P('seg', 'src'), may hold values from 0 to 1
- huber_weight: float32 [8, 524288], P('seg', 'src'), may hold values from 0.1 to 1
- residual: float32 [8, 524288], P('seg', 'src')
- knot_offset: int32 [8, 524288], P('seg', 'src'), may hold values from 0 to 124
- detector_index: int32 [8, 524288], P('seg', 'src'), may hold values from 0 to 61
- calibration_partials: bfloat16 [8, 4, 524288], P('seg', None, 'src'), may hold values from 0.5 to 1.5
- source_index: int32 [8, 524288], P('seg', 'src'), may hold values from 0 to 127
- source_partials: bfloat16 [8, 5, 524288], P('seg', None, 'src')
- send_counts: int32 [8, 32, 32], P('seg', 'src'), may hold values from 0 to 8, as said below
Outputs:
- attitude_step: float32 [8, 4, 4096], P('seg', None, 'src')
- calibration_step: float32 [8, 4, 62], P('seg')
- source_step: float32 [5, 4096], P(None, 'src')
- updated_residual: float32 [8, 524288], P('seg', 'src')
Inputs may be any that keep to these rules, and one draw needn't show every extreme that they name: Each row send_counts[s, q, :] sums to 128; the blocks of a shard are stored in order of owner; in every segment one owner receives exactly 8 blocks from every shard.
All inputs are finite; a program needn't handle non-finite values.
Results may differ from a plain program's by a relative error of at most 0.0003.
Values sent between devices are 32-bit elements; how exact they have to be, the bound alone decides.
A program may use at most 64 MiB of HBM per device.

v0:
```python
import math

import jax
import jax.numpy as jnp
import numpy as np
from jax import lax
from jax.sharding import PartitionSpec as P

SP = 5
CALP = 4
CCDS = 62
BSIZE = 128
ITERS = 6
KN_DEV = 128
S_DEV = 128


highest = lax.Precision.HIGHEST
attitude_prior = 0.5
pair_left = np.array([0, 1, 2, 3, 0, 1, 2, 0, 1, 0])
pair_right = np.array([0, 1, 2, 3, 1, 2, 3, 2, 3, 3])
symmetric_index = np.array([0, 4, 7, 9, 4, 1, 5, 8, 7, 5, 2, 6, 9, 8, 6, 3])
pair_start = (0, 4, 7, 9)
group_blocks = 16
feature_rows = 116
column_target = 8192


def spline_basis(phases):
    rest = 1.0 - phases
    square = phases * phases
    cubed = square * phases
    return jnp.stack(
        [
            rest * rest * rest / 6.0,
            (3.0 * cubed - 6.0 * square + 4.0) / 6.0,
            (-3.0 * cubed + 3.0 * square + 3.0 * phases + 1.0) / 6.0,
            cubed / 6.0,
        ],
        0,
    )


def row_features(partials, phases, weight, residual_now):
    columns = phases.shape[-1]
    spline = spline_basis(phases)
    basis_pairs = spline[pair_left] * spline[pair_right]
    outer_partials = partials[pair_left] * partials[pair_right]
    products = ((weight * basis_pairs)[:, None, :] * outer_partials[None]).reshape(100, columns)
    right_terms = ((weight * residual_now * spline)[:, None, :] * partials[None]).reshape(
        16, columns
    )
    return (jnp.concatenate([products, right_terms], 0), spline)


def shift_knots(values, shift_amount):
    if shift_amount == 0:
        return values
    padding = jnp.zeros(values.shape[:-1] + (abs(shift_amount),), values.dtype)
    if shift_amount > 0:
        return jnp.concatenate([padding, values[..., :-shift_amount]], axis=-1)
    return jnp.concatenate([values[..., -shift_amount:], padding], axis=-1)


def normal_system(totals):
    span_knots = totals.shape[-1]
    compact = totals[:100].reshape(10, 10, span_knots)
    products = compact[:, symmetric_index].reshape(10, 4, 4, span_knots)
    right_terms = totals[100:].reshape(4, 4, span_knots)
    blocks = []
    for d in range(4):
        summed = products[pair_start[d]]
        for i in range(1, 4 - d):
            summed = summed + shift_knots(products[pair_start[d] + i], i)
        blocks.append(summed)
    right_side = right_terms[0]
    for i in range(1, 4):
        right_side = right_side + shift_knots(right_terms[i], i)
    return (blocks, right_side)


def apply_normal(blocks, values):
    result = attitude_prior * values + jnp.einsum(
        "jlk,lk->jk", blocks[0], values, precision=highest
    )
    for d in range(1, 4):
        result = result + jnp.einsum(
            "jlk,lk->jk", blocks[d], shift_knots(values, -d), precision=highest
        )
        result = result + shift_knots(
            jnp.einsum("jlk,jk->lk", blocks[d], values, precision=highest), d
        )
    return result


def solve_attitude(totals):
    blocks, right_side = normal_system(totals)
    diagonal = jnp.stack([blocks[0][j, j] for j in range(4)], 0) + attitude_prior
    solution = jnp.zeros_like(right_side)
    remaining = right_side
    scaled = remaining / diagonal
    direction = scaled
    precond_norm = jnp.sum(remaining * scaled)
    for step_index in range(ITERS):
        product_image = apply_normal(blocks, direction)
        step_length = precond_norm / jnp.sum(direction * product_image)
        solution = solution + step_length * direction
        remaining = remaining - step_length * product_image
        scaled = remaining / diagonal
        norm_next = jnp.sum(remaining * scaled)
        direction = scaled + norm_next / precond_norm * direction
        precond_norm = norm_next
    return solution


def knot_table(solution):
    shifted = [shift_knots(solution, -i) for i in range(4)]
    stacked = jnp.stack(shifted, axis=-3)
    return stacked.reshape(solution.shape[:-2] + (16, solution.shape[-1]))


def correction(spline, partials, values_at):
    grid = values_at.reshape((4, 4) + values_at.shape[1:])
    return jnp.sum(spline[:, None] * partials[None] * grid, axis=(0, 1))


def knot_hot(offsets, span_knots):
    return (offsets[..., None] == jnp.arange(span_knots, dtype=jnp.int32)).astype(jnp.float32)


def build_rows(partials, phases, weight, residual_now, offsets, counts, starts, capacity):
    span = capacity * BSIZE
    stacked = jnp.concatenate(
        [partials.astype(jnp.float32), phases[None], weight[None], residual_now[None]], 0
    )
    stacked = jnp.pad(stacked, ((0, 0), (0, span)))
    padded_knots = jnp.pad(offsets, (0, span))

    def window(start_block):
        first = start_block * BSIZE
        return (
            lax.dynamic_slice_in_dim(stacked, first, span, 1),
            lax.dynamic_slice_in_dim(padded_knots, first, span, 0),
        )

    outgoing, out_knots = jax.vmap(window, out_axes=(1, 0))(starts)
    valid = jnp.arange(span, dtype=jnp.int32)[None, :] < counts[:, None] * BSIZE
    keep = jnp.logical_or(jnp.arange(7)[:, None, None] != 5, valid[None])
    outgoing = jnp.where(keep, outgoing, 0.0)
    return (outgoing, out_knots[None])


def sender_groups(received):
    senders = received.shape[1]
    span = received.shape[2]
    together = math.gcd(senders, max(1, column_target // span))
    return (senders // together, together, span)


def owner_assembly(received, recv_knots):
    steps_count, together, span = sender_groups(received)

    def add_senders(step_index, totals):
        first = step_index * together
        grouped = lax.dynamic_slice_in_dim(received, first, together, 1).reshape(7, together * span)
        group_knots = lax.dynamic_slice_in_dim(recv_knots[0], first, together, 0).reshape(
            together * span
        )
        features, unused = row_features(grouped[:4], grouped[4], grouped[5], grouped[6])
        return totals + jnp.dot(features, knot_hot(group_knots, KN_DEV), precision=highest)

    return lax.fori_loop(
        0, steps_count, add_senders, jnp.zeros((feature_rows, KN_DEV), jnp.float32)
    )


def owner_corrections(solution, received, recv_knots):
    steps_count, together, span = sender_groups(received)
    table_now = knot_table(solution)

    def one_step(step_index):
        first = step_index * together
        grouped = lax.dynamic_slice_in_dim(received, first, together, 1).reshape(7, together * span)
        group_knots = lax.dynamic_slice_in_dim(recv_knots[0], first, together, 0).reshape(
            together * span
        )
        values_at = jnp.dot(table_now, knot_hot(group_knots, KN_DEV).T, precision=highest)
        spline = spline_basis(grouped[4])
        return correction(spline, grouped[:4], values_at).reshape(together, span)

    results = lax.map(one_step, jnp.arange(steps_count, dtype=jnp.int32))
    return results.reshape(received.shape[1], span)


def body(
    attitude_partials,
    scan_phase,
    huber_weight,
    residual,
    knot_offset,
    detector_index,
    calibration_partials,
    source_index,
    source_partials,
    send_counts,
):
    partials = attitude_partials[0]
    phases = scan_phase[0]
    weight = huber_weight[0]
    residual_now = residual[0]
    offsets = knot_offset[0]
    transits_here = phases.shape[0]
    blocks = transits_here // BSIZE
    shards = lax.axis_size("src")
    capacity = 2 * blocks // shards
    group_rows = group_blocks * BSIZE
    counts = send_counts[0, 0]
    run_ends = jnp.cumsum(counts)
    starts = run_ends - counts
    block_ids = jnp.arange(blocks, dtype=jnp.int32)
    block_owner = jnp.sum((run_ends[None, :] <= block_ids[:, None]).astype(jnp.int32), axis=1)
    owner_match = block_owner[:, None] == jnp.arange(shards, dtype=jnp.int32)[None, :]
    block_slot = block_ids - jnp.sum(jnp.where(owner_match, starts[None, :], 0), axis=1)
    outgoing, out_knots = build_rows(
        partials, phases, weight, residual_now, offsets, counts, starts, capacity
    )
    received, recv_knots = (
        lax.all_to_all(outgoing, "src", split_axis=1, concat_axis=1, tiled=True),
        lax.all_to_all(out_knots, "src", split_axis=1, concat_axis=1, tiled=True),
    )
    solution = solve_attitude(owner_assembly(received, recv_knots))
    owner_values = owner_corrections(solution, received, recv_knots)
    returned = lax.all_to_all(owner_values, "src", split_axis=0, concat_axis=0, tiled=True)
    slot_index = block_owner * capacity + block_slot
    corrections_here = jnp.take(
        returned.reshape(shards * capacity, BSIZE), slot_index, axis=0
    ).reshape(transits_here)
    updated = residual_now - corrections_here
    detectors = detector_index[0]
    sources = source_index[0]
    calibration = calibration_partials[0]
    source_terms = source_partials[0]

    def add_sums(group_index, carried):
        calib_totals, source_totals = carried
        first = group_index * group_rows
        group_weight = lax.dynamic_slice_in_dim(weight, first, group_rows, 0)
        group_updated = lax.dynamic_slice_in_dim(updated, first, group_rows, 0)
        group_calib = lax.dynamic_slice_in_dim(calibration, first, group_rows, 1).astype(
            jnp.float32
        )
        group_source = lax.dynamic_slice_in_dim(source_terms, first, group_rows, 1).astype(
            jnp.float32
        )
        calib_features = jnp.concatenate(
            [group_weight * group_updated * group_calib, group_weight * group_calib * group_calib],
            0,
        )
        source_features = jnp.concatenate(
            [
                group_weight * group_updated * group_source,
                group_weight * group_source * group_source,
            ],
            0,
        )
        ccd_hot = knot_hot(lax.dynamic_slice_in_dim(detectors, first, group_rows, 0), CCDS)
        source_hot = knot_hot(lax.dynamic_slice_in_dim(sources, first, group_rows, 0), S_DEV)
        calib_totals = calib_totals + jnp.dot(calib_features, ccd_hot, precision=highest)
        source_totals = source_totals + jnp.dot(source_features, source_hot, precision=highest)
        return (calib_totals, source_totals)

    calib_totals, source_totals = lax.fori_loop(
        0,
        transits_here // group_rows,
        add_sums,
        (jnp.zeros((2 * CALP, CCDS), jnp.float32), jnp.zeros((2 * SP, S_DEV), jnp.float32)),
    )
    calib_summed = lax.psum(calib_totals, "src")
    source_summed = lax.psum(source_totals, "seg")
    calib_result = calib_summed[:CALP] / (1.0 + calib_summed[CALP:])
    source_result = source_summed[:SP] / (1.0 + source_summed[SP:])
    return (solution[None], calib_result[None], source_result, updated[None])


def solution(mesh):
    return jax.shard_map(
        body,
        mesh=mesh,
        in_specs=(
            P("seg", None, "src"),
            P("seg", "src"),
            P("seg", "src"),
            P("seg", "src"),
            P("seg", "src"),
            P("seg", "src"),
            P("seg", None, "src"),
            P("seg", "src"),
            P("seg", None, "src"),
            P("seg", "src", None),
        ),
        out_specs=(P("seg", None, "src"), P("seg", None, None), P(None, "src"), P("seg", "src")),
        check_vma=False,
    )
```

profile of v0, /device:TPU:1, one launch (start us, length us, event | category | flops | bytes accessed | tf_op | source)
XLA Modules:
  0.0 408.6 jit_solution(6180224304958648568)
XLA Ops:
  2.4 42.5 %while.46 = (s32[]{:T(128)}, s32[17408]{0:T(1024)S(1)}, s32[32,1]{1,0:T(8,128)S(1)}, s32[32,1024]{1,0:T(8,128)S(1)}, s32[]{:T(128)}, /*index=5*/s32[]{:T(128)}) while((s32[]{:T(128)}, s32[17408]{0:T(1024)S(1)}, s32[32,1]{1,0:T(8,128)S(1)}, s32[32,1024]{1,0:T(8,128)S(1)}, s32[]{:T(128)}, /*index=5*/s32[]{:T(128)}) %tuple.190), condition=%wide.while_cond.1, body=%wide.while_body.1.sunk | while | flops 2 | bytes 16473 | solution.py:143
  45.7 8.6 %all-to-all-start.1 = ((s32[1,32,1024]{2,0,1:T(1,128)}), s32[1,32,1024]{2,0,1:T(1,128)S(1)}, u32[]{:S(2)}, u32[]{:S(2)}) async-start(s32[1,32,1024]{2,0,1:T(1,128)} %broadcast_in_dim.122), calls=%async_computation.1 | async-start | bytes 262144 | tf_op jit(solution)/shard_map/all_to_all | solution.py:229
  55.1 0.9 bitcast_convert_fusion
  56.1 1.2 select_maximum_fusion
  57.2 42.2 %while.45 = (s32[]{:T(128)}, f32[7,17408]{1,0:T(8,128)S(1)}, s32[32,2]{1,0:T(8,128)S(1)}, f32[32,7,1024]{2,1,0:T(8,128)S(1)}, s32[]{:T(128)}) while((s32[]{:T(128)}, f32[7,17408]{1,0:T(8,128)S(1)}, s32[32,2]{1,0:T(8,128)S(1)}, f32[32,7,1024]{2,1,0:T(8,128)S(1)}, s32[]{:T(128)}) %tuple.187), condition=%wide.while_cond, body=%wide.while_body.sunk | while | flops 2 | bytes 65633 | solution.py:142
  99.4 1.2 bitcast_select_fusion
  100.6 7.4 %all-to-all-start = ((f32[7,32,1024]{2,0,1:T(8,128)}), f32[7,32,1024]{2,0,1:T(8,128)S(1)}, u32[]{:S(2)}, u32[]{:S(2)}) async-start(f32[7,32,1024]{2,0,1:T(8,128)} %bitcast_select_fusion), calls=%async_computation | async-start | bytes 2097152 | tf_op jit(solution)/shard_map/all_to_all | solution.py:228
  108.9 16.0 %all-to-all-done = f32[7,32,1024]{2,0,1:T(8,128)S(1)} async-done(((f32[7,32,1024]{2,0,1:T(8,128)}), f32[7,32,1024]{2,0,1:T(8,128)S(1)}, u32[]{:S(2)}, u32[]{:S(2)}) %all-to-all-start) | async-done | bytes 917536 | tf_op jit(solution)/shard_map/all_to_all | solution.py:228
  124.9 1.5 copy.51
  126.4 83.4 %while.48 = (s32[]{:T(128)}, f32[116,128]{1,0:T(8,128)}, f32[7,32,1024]{2,1,0:T(8,128)}, s32[1,32,1024]{2,1,0:T(8,128)}, s32[]{:T(128)}, /*index=5*/s32[]{:T(128...) while((s32[]{:T(128)}, f32[116,128]{1,0:T(8,128)}, ...), condition=%wide.region_2.3_spmd.clone.clone.clone, body=%wide.region_1.2_spmd.sunk.clone.clone.clone.sunk | while | flops 1463139328 | bytes 22573536 | solution.py:172
  129.7 0.9 dynamic-slice_bitcast_fusion.18
  132.1 2.9 broadcast_multiply_fusion.11
  135.0 3.3 mul.1153
  138.3 1.8 broadcast_multiply_fusion.10
  140.1 2.0 mul.1151
  142.9 4.4 %fusion.77 = f32[116,128]{1,0:T(8,128)} fusion(s32[8192]{0:T(1024)S(1)} %bitcast.503, f32[16,8192]{1,0:T(8,128)} %mul.1151, f32[100,8192]{1,0:T(8,128)S(1)} %mul.1153, f32[116,128]{1,0:T(8,128)} %get-tuple-element.917, pred[]{:T(512)S(6)} %compare.69), kind=kOutput, calls=%fused_computation.53.clone.1 | convolution fusion | flops 1461646336 | bytes 3952641 | tf_op jit(solution)/shard_map/while/body/eval_jaxpr/dot_general | solution.py:170
  150.6 0.9 dynamic-slice_bitcast_fusion.18
  153.0 2.9 broadcast_multiply_fusion.11
  155.9 3.3 mul.1153
  159.1 1.8 broadcast_multiply_fusion.10
  160.9 2.0 mul.1151
  163.7 4.4 %fusion.77 = f32[116,128]{1,0:T(8,128)} fusion(s32[8192]{0:T(1024)S(1)} %bitcast.503, f32[16,8192]{1,0:T(8,128)} %mul.1151, f32[100,8192]{1,0:T(8,128)S(1)} %mul.1153, f32[116,128]{1,0:T(8,128)} %get-tuple-element.917, pred[]{:T(512)S(6)} %compare.69), kind=kOutput, calls=%fused_computation.53.clone.1 | convolution fusion | flops 1461646336 | bytes 3952641 | tf_op jit(solution)/shard_map/while/body/eval_jaxpr/dot_general | solution.py:170
  171.4 0.9 dynamic-slice_bitcast_fusion.18
  173.8 2.9 broadcast_multiply_fusion.11
  176.7 3.3 mul.1153
  180.0 1.8 broadcast_multiply_fusion.10
  181.8 2.0 mul.1151
  184.6 4.4 %fusion.77 = f32[116,128]{1,0:T(8,128)} fusion(s32[8192]{0:T(1024)S(1)} %bitcast.503, f32[16,8192]{1,0:T(8,128)} %mul.1151, f32[100,8192]{1,0:T(8,128)S(1)} %mul.1153, f32[116,128]{1,0:T(8,128)} %get-tuple-element.917, pred[]{:T(512)S(6)} %compare.69), kind=kOutput, calls=%fused_computation.53.clone.1 | convolution fusion | flops 1461646336 | bytes 3952641 | tf_op jit(solution)/shard_map/while/body/eval_jaxpr/dot_general | solution.py:170
  192.2 0.9 dynamic-slice_bitcast_fusion.18
  194.6 2.9 broadcast_multiply_fusion.11
  197.5 3.3 mul.1153
  200.8 1.8 broadcast_multiply_fusion.10
  202.6 2.0 mul.1151
  205.4 4.4 %fusion.77 = f32[116,128]{1,0:T(8,128)} fusion(s32[8192]{0:T(1024)S(1)} %bitcast.503, f32[16,8192]{1,0:T(8,128)} %mul.1151, f32[100,8192]{1,0:T(8,128)S(1)} %mul.1153, f32[116,128]{1,0:T(8,128)} %get-tuple-element.917, pred[]{:T(512)S(6)} %compare.69), kind=kOutput, calls=%fused_computation.53.clone.1 | convolution fusion | flops 1461646336 | bytes 3952641 | tf_op jit(solution)/shard_map/while/body/eval_jaxpr/dot_general | solution.py:170
  239.0 32.4 %while.44 = (s32[]{:T(128)}, f32[4,8,1024]{2,1,0:T(8,128)}, s32[4]{0:T(128)S(1)}, f32[7,32,1024]{2,1,0:T(8,128)}, s32[1,32,1024]{2,1,0:T(8,128)}, /*index=5*/f32...) while((s32[]{:T(128)}, f32[4,8,1024]{2,1,0:T(8,128)}, ...), condition=%wide.region_19.20_spmd, body=%wide.region_17.19_spmd.sunk | while | flops 203014144 | bytes 3777219 | solution.py:191
  243.4 3.0 fusion.72
  249.4 0.9 dynamic-slice_bitcast_fusion.14
  251.5 3.0 fusion.72
  257.5 0.9 dynamic-slice_bitcast_fusion.14
  259.6 3.0 fusion.72
  265.6 0.9 dynamic-slice_bitcast_fusion.14
  267.7 3.0 fusion.72
  271.3 1.7 all_to_all.14
  273.0 4.0 all-to-all-start.2
  277.1 7.6 %all-to-all-done.2 = f32[32,1,1024]{2,1,0:T(1,128)S(1)} async-done(((f32[32,1,1024]{2,1,0:T(1,128)}), f32[32,1,1024]{2,1,0:T(1,128)S(1)}, u32[]{:S(2)}, u32[]{:S(2)}) %all-to-all-start.2) | async-done | bytes 131104 | tf_op jit(solution)/shard_map/all_to_all | solution.py:233
  286.1 38.6 %while.47 = (s32[]{:T(128)}, f32[8,62]{1,0:T(8,128)S(1)}, f32[10,128]{1,0:T(8,128)S(1)}, f32[16384]{0:T(1024)}, f32[16384]{0:T(1024)S(1)}, /*index=5*/bf16[4,163...) while((s32[]{:T(128)}, f32[8,62]{1,0:T(8,128)S(1)}, ...), condition=%wide.region_21.22_spmd.clone, body=%wide.region_20.21_spmd.clone.sunk | while | flops 44152296 | bytes 460874 | solution.py:272
  324.7 16.5 %psum.15 = f32[10,128]{1,0:T(8,128)S(1)} all-reduce(f32[10,128]{1,0:T(8,128)S(1)} %get-tuple-element.363), channel_id=1, replica_groups=mesh['seg'=8,'src'=32] {'seg'}, use_global_device_ids=true, to_apply=%region_23.24 | all-reduce | flops 1280 | bytes 10240 | tf_op jit(solution)/shard_map/psum | solution.py:279
  341.8 66.2 %psum.14 = f32[8,62]{1,0:T(8,128)S(1)} all-reduce(f32[8,62]{1,0:T(8,128)S(1)} %get-tuple-element.362), channel_id=1, replica_groups=mesh['seg'=8,'src'=32] {'src'}, use_global_device_ids=true, to_apply=%region_22.23 | all-reduce | flops 496 | bytes 3968 | tf_op jit(solution)/shard_map/psum | solution.py:278
  (511 shorter events, 179.7 us)
Async XLA Ops:
  0.6 107.4 %copy-start.4 = (s32[16]{0:T(128)S(1)}, s32[16]{0:T(128)}, u32[]{:S(2)}) copy-start(s32[16]{0:T(128)} %constant.350) | copy-start | bytes 196
  45.7 54.9 %all-to-all-start.1 = ((s32[1,32,1024]{2,0,1:T(1,128)}), s32[1,32,1024]{2,0,1:T(1,128)S(1)}, u32[]{:S(2)}, u32[]{:S(2)}) async-start(s32[1,32,1024]{2,0,1:T(1,128)} %broadcast_in_dim.122), calls=%async_computation.1 | async-start | bytes 262144 | tf_op jit(solution)/shard_map/all_to_all | solution.py:229
  55.0 71.4 %copy-start.2 = (s32[10]{0:T(128)S(1)}, s32[10]{0:T(128)}, u32[]{:S(2)}) copy-start(s32[10]{0:T(128)} %constant.662) | copy-start | bytes 124
  55.0 71.4 %copy-start.3 = (s32[10]{0:T(128)S(1)}, s32[10]{0:T(128)}, u32[]{:S(2)}) copy-start(s32[10]{0:T(128)} %constant.663) | copy-start | bytes 124
  100.6 24.3 %all-to-all-start = ((f32[7,32,1024]{2,0,1:T(8,128)}), f32[7,32,1024]{2,0,1:T(8,128)S(1)}, u32[]{:S(2)}, u32[]{:S(2)}) async-start(f32[7,32,1024]{2,0,1:T(8,128)} %bitcast_select_fusion), calls=%async_computation | async-start | bytes 2097152 | tf_op jit(solution)/shard_map/all_to_all | solution.py:228
  108.1 18.3 %copy-start.5 = (s32[128]{0:T(128)}, s32[128]{0:T(128)S(1)}, u32[]{:S(2)}) copy-start(s32[128]{0:T(128)S(1)} %convert_reduce_fusion) | copy-start | bytes 1540
  108.2 18.2 %copy-start.7 = (s32[128]{0:T(128)}, s32[128]{0:T(128)S(1)}, u32[]{:S(2)}) copy-start(s32[128]{0:T(128)S(1)} %select_reduce_fusion) | copy-start | bytes 1540
  238.4 0.6 copy-start.1
  238.7 38.3 %copy-start.6 = (s32[128]{0:T(128)S(1)}, s32[128]{0:T(128)}, u32[]{:S(2)}) copy-start(s32[128]{0:T(128)} %copy-done.5) | copy-start | bytes 1540
  238.7 38.3 %copy-start.8 = (s32[128]{0:T(128)S(1)}, s32[128]{0:T(128)}, u32[]{:S(2)}) copy-start(s32[128]{0:T(128)} %copy-done.7) | copy-start | bytes 1540
  238.7 46.7 %copy-start = (f32[1,16384]{1,0:T(1,128)S(1)}, f32[1,16384]{1,0:T(1,128)}, u32[]{:S(2)}) copy-start(f32[1,16384]{1,0:T(1,128)} %param.27) | copy-start | bytes 196612
  273.0 11.7 %all-to-all-start.2 = ((f32[32,1,1024]{2,1,0:T(1,128)}), f32[32,1,1024]{2,1,0:T(1,128)S(1)}, u32[]{:S(2)}, u32[]{:S(2)}) async-start(f32[32,1,1024]{2,1,0:T(1,128)} %all_to_all.14), calls=%async_computation.2 | async-start | bytes 262144 | tf_op jit(solution)/shard_map/all_to_all | solution.py:233
where the time goes:
time: 414 us; the launch traced here: 409 us
  local copies, waits for them, and re-layouts  166 us (40%)
  blocking collectives  82.7 us (20%)
  other arithmetic  57.7 us (14%)
  matrix products  38.8 us (9%)
  waiting for transfers between devices  23.6 us (6%)
  starting transfers between devices  19.9 us (5%)
  between operations  15.8 us (4%)
  loops' own time  4.5 us (1%)
    gather x192, local copies, waits for them, and re-layouts  83.8 us
    psum x1, blocking collectives, body(): calib_summed = lax.psum(calib_totals, 'src')  66.2 us
    while x52, local copies, waits for them, and re-layouts  20.9 us
    dot_general x4, matrix products, add_senders(): jnp.dot(features, knot_hot(group_knots, KN_DEV), precision=highest)  17.5 us
    psum x1, blocking collectives, body(): source_summed = lax.psum(source_totals, 'seg')  16.5 us
    all_to_all x1, waiting for transfers between devices, body(): lax.all_to_all(outgoing, 'src', split_axis=1, concat_axis=1, tiled=True)  16 us
    mul x4, local copies, waits for them, and re-layouts, row_features(): (weight * basis_pairs)[:, None, :] * outer_partials[None]  13 us
    dot_general x4, matrix products, one_step(): jnp.dot(table_now, knot_hot(group_knots, KN_DEV).T, precision=highest)  12 us
  transfers between devices with their start and end apart: 3, of which 2 were waited for; matrix products, arithmetic and copies ran while one was open for 12% of the time, Pallas kernels for 0%

commit v1 on v0

v1 whole, which is shorter than its diff:
```python
import functools

import jax
import jax.numpy as jnp
from jax import lax
from jax.experimental import pallas as pl
from jax.experimental.pallas import tpu as pltpu
from jax.sharding import PartitionSpec as P

SP = 5
CALP = 4
CCDS = 62
BSIZE = 128
ITERS = 6
LANES = 128
GROUP = 8
PACKED = 48
attitude_prior = 0.5
f32 = jnp.float32
bf16 = jnp.bfloat16
MESH = pl.DeviceIdType.MESH
VMEM = pltpu.VMEM
nt = (((1,), (1,)), ((), ()))

pairs = [(d, i) for d in range(4) for i in range(4 - d)]


def spline_basis(u):
    rest = 1.0 - u
    square = u * u
    cubed = square * u
    return [
        rest * rest * rest / 6.0,
        (3.0 * cubed - 6.0 * square + 4.0) / 6.0,
        (-3.0 * cubed + 3.0 * square + 3.0 * u + 1.0) / 6.0,
        cubed / 6.0,
    ]


def row_ids():
    return lax.broadcasted_iota(jnp.int32, (8, LANES), 0)


def split_two(x):
    high = x.astype(bf16)
    return high, (x - high.astype(f32)).astype(bf16)


def spread(ref, row, rows=8):
    return jnp.broadcast_to(ref[pl.ds(row, 1), :], (rows, LANES))


def one_hot(index_rows, count):
    ids = lax.broadcasted_iota(jnp.int32, (count, LANES), 0).astype(f32).astype(bf16)
    picked = jnp.broadcast_to(index_rows, (count, LANES)).astype(bf16)
    return jnp.where(picked == ids, jnp.ones((), bf16), jnp.zeros((), bf16))


def fill_owners(counts_ref, owner_ref, owners, blocks, capacity):
    start = jnp.int32(0)
    for o in range(owners):
        for c in range(capacity):
            owner_ref[start + c] = jnp.int32(o)
        start = start + counts_ref[0, o]


def twice(x):
    return jnp.concatenate([x, x], axis=0)


def assemble_kernel(
    owners, capacity, counts_ref, part_ref, phase_ref, weight_ref, resid_ref, offset_ref,
    out_ref, owner_ref, rows_ref, acc_ref,
):
    blocks = phase_ref.shape[0]
    stride = 64
    fill_owners(counts_ref, owner_ref, owners, blocks, capacity)
    acc_ref[...] = jnp.zeros_like(acc_ref)
    rows_ref[...] = jnp.zeros_like(rows_ref)
    low = row_ids() < 4

    def group_step(group, carry):
        base = pl.multiple_of(group * GROUP, GROUP)
        here = pl.ds(base, GROUP)
        spline = spline_basis(phase_ref[here, :])
        weight = weight_ref[here, :]
        weighted = [weight * s for s in spline]
        resid = resid_ref[here, :]

        def put(row, value):
            rows_ref[pl.ds(row, GROUP, stride=stride), :] = value

        for p, (d, i) in enumerate(pairs):
            value = weighted[i] * spline[i + d]
            put(p, value)
            put(16 + 8 * i + 2 * d, value)
            put(16 + 8 * i + 2 * d + 1, value)
        put(10, offset_ref[here, :].astype(f32))
        for i in range(4):
            value = weighted[i] * resid
            for j in range(4):
                put(48 + 4 * i + j, value)
        for q in range(GROUP):
            first = q * stride
            lanes = pl.ds(pl.multiple_of((base + q) * BSIZE, BSIZE), BSIZE)
            a8 = twice(part_ref[0, :, lanes].astype(f32))
            main = a8 * jnp.where(low, a8, pltpu.roll(a8, 7, 0))
            cross = a8 * pltpu.roll(a8, 6, 0)
            features = [main * spread(rows_ref, first + p) for p in range(10)]
            features += [cross * rows_ref[pl.ds(first + 16 + 8 * i, 8), :] for i in range(4)]
            features += [a8 * rows_ref[pl.ds(first + 48 + 8 * h, 8), :] for h in range(2)]
            high, rest = split_two(jnp.concatenate(features, axis=0))
            hot = one_hot(rows_ref[pl.ds(first + 10, 1), :], LANES)
            summed = lax.dot_general(
                jnp.concatenate([high, rest], axis=1), jnp.concatenate([hot, hot], axis=1),
                nt, preferred_element_type=f32,
            )
            owner = owner_ref[base + q]
            acc_ref[owner] = acc_ref[owner] + summed
        return carry

    lax.fori_loop(0, blocks // GROUP, group_step, 0)

    def pack_chip(chip, carry):
        for core in range(2):
            tiles = acc_ref.at[2 * chip + core]

            def shifted(t, i):
                tile = tiles[pl.ds(8 * t, 8), :]
                return tile if i == 0 else pltpu.roll(tile, i, 1)

            for d in range(4):
                total = None
                for p, (pd, i) in enumerate(pairs):
                    if pd == d:
                        term = shifted(p, i)
                        total = term if total is None else total + term
                out_ref[core, chip, pl.ds(8 * d, 8), :] = total
            out_ref[core, chip, pl.ds(32, 8), :] = (
                (shifted(10, 0) + shifted(11, 1)) + (shifted(12, 2) + shifted(13, 3))
            )
            out_ref[core, chip, pl.ds(40, 8), :] = jnp.where(
                low, shifted(14, 0), shifted(14, 1)
            ) + jnp.where(low, shifted(15, 2), shifted(15, 3))
        return carry

    lax.fori_loop(0, owners // 2, pack_chip, 0)


def total_of(x):
    return jnp.sum(jnp.sum(x, axis=1, keepdims=True), axis=0, keepdims=True)


def solve_owner(tiles):
    low = row_ids() < 4
    right_side = tiles[5] + pltpu.roll(tiles[5], 4, 0)
    cross = tiles[4]
    coefficients = []
    for d in range(4):
        first = tiles[d]
        pair_now = cross[2 * d : 2 * d + 2]
        second = jnp.concatenate([pair_now, pair_now, first[7:8], first[4:7]], axis=0)
        if d == 0:
            first = jnp.where(low, first + attitude_prior, first)
            coefficients.append((0, first, second))
            diagonal = jnp.where(low, first, pltpu.roll(first, 4, 0))
        else:
            coefficients.append((d, first, second))
            coefficients.append((-d, pltpu.roll(first, d, 1), pltpu.roll(second, d, 1)))

    def apply_normal(p):
        near = jnp.where(low, p, pltpu.roll(p, 7, 0))
        far = jnp.where(low, pltpu.roll(p, 6, 0), pltpu.roll(p, 5, 0))
        terms = []
        for d, first, second in coefficients:
            if d == 0:
                terms.append(first * near + second * far)
            else:
                shift = (LANES - d) % LANES
                terms.append(first * pltpu.roll(near, shift, 1) + second * pltpu.roll(far, shift, 1))
        result = ((terms[0] + terms[1]) + (terms[2] + terms[3])) + (
            (terms[4] + terms[5]) + terms[6]
        )
        return result + pltpu.roll(result, 4, 0)

    step = jnp.zeros_like(right_side)
    remaining = right_side
    scaled = remaining / diagonal
    direction = scaled
    norm = total_of(remaining * scaled)
    for iteration in range(ITERS):
        image = apply_normal(direction)
        length = norm / total_of(direction * image)
        step = step + length * direction
        if iteration + 1 < ITERS:
            remaining = remaining - length * image
            scaled = remaining / diagonal
            norm_next = total_of(remaining * scaled)
            direction = scaled + norm_next / norm * direction
            norm = norm_next
    return step


def loop(lower, upper, step):
    def run(k, carry):
        step(k)
        return carry

    lax.fori_loop(lower, upper, run, 0)


def exchange_kernel(
    owners, parts_ref, out_ref, got_pair, mine, got_chip, got_step,
    pair_send, pair_recv, chip_send, chip_recv, step_send, step_recv,
):
    chips = owners // 2
    me = lax.axis_index("src")
    core = lax.rem(me, 2)
    chip = me // 2
    partner = me + 1 - 2 * core
    barrier = pltpu.get_barrier_semaphore()

    def greet(k):
        pl.semaphore_signal(
            barrier, inc=1, device_id={"src": lax.rem(me + k, owners)}, device_id_type=MESH
        )

    loop(1, owners, greet)
    pl.semaphore_wait(barrier, owners - 1)

    def pair_copy(k):
        target_chip = lax.rem(chip + k, chips)
        return pltpu.make_async_remote_copy(
            src_ref=parts_ref.at[1 - core, target_chip], dst_ref=got_pair.at[k],
            send_sem=pair_send.at[k], recv_sem=pair_recv.at[k],
            device_id={"src": partner}, device_id_type=MESH,
        )

    def chip_copy(k):
        return pltpu.make_async_remote_copy(
            src_ref=mine.at[k], dst_ref=got_chip.at[k],
            send_sem=chip_send.at[k], recv_sem=chip_recv.at[k],
            device_id={"src": 2 * lax.rem(chip + k, chips) + core}, device_id_type=MESH,
        )

    loop(1, chips, lambda k: pair_copy(k).start())
    pair_copy(0).start()

    def add_pair(k):
        pair_copy(k).wait_recv()
        mine[k] = parts_ref[core, lax.rem(chip + k, chips)] + got_pair[k]

    add_pair(1)

    def add_and_send(k):
        add_pair(k)
        chip_copy(k - 1).start()

    loop(2, chips, add_and_send)
    add_pair(0)
    chip_copy(chips - 1).start()

    def gather(k, total):
        chip_copy(k).wait_recv()
        return total + got_chip[k]

    total = lax.fori_loop(1, chips, gather, mine[0])
    step = solve_owner([total[8 * t : 8 * t + 8] for t in range(PACKED // 8)])
    got_step[me] = step[0:4]

    def step_copy(k, slot):
        return pltpu.make_async_remote_copy(
            src_ref=got_step.at[slot], dst_ref=got_step.at[slot],
            send_sem=step_send.at[k], recv_sem=step_recv.at[slot],
            device_id={"src": lax.rem(me + k, owners)}, device_id_type=MESH,
        )

    loop(1, owners, lambda k: step_copy(k, me).start())

    def drain(k):
        pair_copy(k).wait_send()
        chip_copy(k).wait_send()

    loop(1, chips, drain)
    pair_copy(0).wait_send()
    loop(1, owners, lambda k: step_copy(k, lax.rem(me + k, owners)).wait_recv())
    out_ref[...] = got_step[...]
    loop(1, owners, lambda k: step_copy(k, me).wait_send())


def correct_kernel(
    owners, owner_ref, steps_ref, part_ref, phase_ref, weight_ref, resid_ref, offset_ref,
    detector_ref, calib_ref, source_ref, sterm_ref,
    updated_ref, calsum_ref, srcsum_ref, rows_ref, table_ref, acc_ref,
):
    blocks = phase_ref.shape[0]
    stride = 24
    rows = row_ids()
    low = rows < 4

    def make_table(o, carry):
        x8 = twice(steps_ref[o])
        table = jnp.concatenate(
            [
                jnp.where(low, x8, pltpu.roll(x8, LANES - 1, 1)),
                jnp.where(low, pltpu.roll(x8, LANES - 2, 1), pltpu.roll(x8, LANES - 3, 1)),
            ],
            axis=0,
        )
        high, rest = split_two(table)
        table_ref[o] = jnp.concatenate([high, rest], axis=0)
        return carry

    lax.fori_loop(0, owners, make_table, 0)
    acc_ref[...] = jnp.zeros_like(acc_ref)

    def group_step(group, carry):
        base = pl.multiple_of(group * GROUP, GROUP)
        here = pl.ds(base, GROUP)
        spline = spline_basis(phase_ref[here, :])

        def put(row, value):
            rows_ref[pl.ds(row, GROUP, stride=stride), :] = value

        put(0, offset_ref[here, :].astype(f32))
        put(1, source_ref[here, :].astype(f32))
        put(2, detector_ref[here, :].astype(f32))
        put(3, weight_ref[here, :])
        put(4, resid_ref[here, :])
        for i in range(4):
            for j in range(4):
                put(8 + 4 * i + j, spline[i])
        lefts = []
        rights = []
        for q in range(GROUP):
            first = q * stride
            lanes = pl.ds(pl.multiple_of((base + q) * BSIZE, BSIZE), BSIZE)
            a8 = twice(part_ref[0, :, lanes].astype(f32))
            hot = one_hot(rows_ref[pl.ds(first, 1), :], LANES)
            values = jnp.dot(table_ref[owner_ref[base + q]], hot, preferred_element_type=f32)
            term = a8 * (
                rows_ref[pl.ds(first + 8, 8), :] * (values[0:8] + values[16:24])
                + rows_ref[pl.ds(first + 16, 8), :] * (values[8:16] + values[24:32])
            )
            term = term + pltpu.roll(term, 4, 0)
            term = term + pltpu.roll(term, 2, 0)
            term = term + pltpu.roll(term, 1, 0)
            updated = spread(rows_ref, first + 4) - term
            updated_ref[pl.ds(base + q, 1), :] = updated[0:1]
            weight = spread(rows_ref, first + 3)
            pull = weight * updated
            sterm = sterm_ref[0, :, lanes].astype(f32)
            eight = jnp.concatenate([sterm[0:4], calib_ref[0, :, lanes].astype(f32)], axis=0)
            fifth = jnp.broadcast_to(sterm[4:5], (8, LANES))
            last = jnp.where(rows == 0, pull, jnp.where(rows == 1, weight * fifth, 0.0)) * fifth
            high, rest = split_two(
                jnp.concatenate([pull * eight, weight * eight * eight, last], axis=0)
            )
            lefts.append(jnp.concatenate([high.astype(f32), rest.astype(f32)], axis=0).astype(bf16))
            rights.append(
                jnp.concatenate(
                    [
                        one_hot(rows_ref[pl.ds(first + 1, 1), :], LANES),
                        one_hot(rows_ref[pl.ds(first + 2, 1), :], LANES),
                    ],
                    axis=0,
                )
            )
        acc_ref[...] += lax.dot_general(
            jnp.concatenate(lefts, axis=1), jnp.concatenate(rights, axis=1), nt,
            preferred_element_type=f32,
        )
        return carry

    lax.fori_loop(0, blocks // GROUP, group_step, 0)
    sums = acc_ref[0:24] + acc_ref[24:48]
    for_source = sums[:, 0:LANES]
    for_calib = sums[:, LANES : 2 * LANES]
    srcsum_ref[0:8] = jnp.concatenate([for_source[0:4], for_source[8:12]], axis=0)
    srcsum_ref[8:16] = for_source[16:24]
    lane = lax.broadcasted_iota(jnp.int32, (4, LANES), 1)
    calsum_ref[...] = jnp.where(lane < 64, for_calib[4:8], pltpu.roll(for_calib, 64, 1)[12:16])


def sums_kernel(
    owners, segments, calsum_ref, srcsum_ref, calib_ref, source_ref, got_cal, got_src,
    cal_send, cal_recv, src_send, src_recv,
):
    me = lax.axis_index("src")
    segment = lax.axis_index("seg")
    barrier = pltpu.get_barrier_semaphore()

    def greet_src(k):
        pl.semaphore_signal(
            barrier, inc=1, device_id={"src": lax.rem(me + k, owners)}, device_id_type=MESH
        )

    def greet_seg(k):
        pl.semaphore_signal(
            barrier, inc=1, device_id={"seg": lax.rem(segment + k, segments)}, device_id_type=MESH
        )

    loop(1, segments, greet_seg)
    loop(1, owners, greet_src)
    pl.semaphore_wait(barrier, owners + segments - 2)

    def src_copy(k, slot):
        return pltpu.make_async_remote_copy(
            src_ref=srcsum_ref, dst_ref=got_src.at[slot],
            send_sem=src_send.at[k], recv_sem=src_recv.at[slot],
            device_id={"seg": lax.rem(segment + k, segments)}, device_id_type=MESH,
        )

    def cal_copy(k, slot):
        return pltpu.make_async_remote_copy(
            src_ref=calsum_ref, dst_ref=got_cal.at[slot],
            send_sem=cal_send.at[k], recv_sem=cal_recv.at[slot],
            device_id={"src": lax.rem(me + k, owners)}, device_id_type=MESH,
        )

    loop(1, segments, lambda k: src_copy(k, segment).start())
    loop(1, owners, lambda k: cal_copy(k, me).start())
    got_src[segment] = srcsum_ref[...]
    got_cal[me] = calsum_ref[...]
    loop(1, segments, lambda k: src_copy(k, lax.rem(segment + k, segments)).wait_recv())
    total = got_src[0]
    for k in range(1, segments):
        total = total + got_src[k]
    source_ref[0:4] = total[0:4] / (1.0 + total[4:8])
    source_ref[4:5] = total[8:9] / (1.0 + total[9:10])
    loop(1, owners, lambda k: cal_copy(k, lax.rem(me + k, owners)).wait_recv())
    total = got_cal[0]
    for k in range(1, owners):
        total = total + got_cal[k]
    result = total / (1.0 + pltpu.roll(total, 64, 1))
    calib_ref[...] = result[:, 0:CCDS]
    loop(1, segments, lambda k: src_copy(k, segment).wait_send())
    loop(1, owners, lambda k: cal_copy(k, me).wait_send())


def body(
    attitude_partials, scan_phase, huber_weight, residual, knot_offset, detector_index,
    calibration_partials, source_index, source_partials, send_counts,
):
    owners = lax.axis_size("src")
    segments = lax.axis_size("seg")
    blocks = scan_phase.shape[1] // BSIZE
    capacity = 2 * blocks // owners
    chips = owners // 2
    spec = pl.BlockSpec(memory_space=VMEM)
    scalars = pl.BlockSpec(memory_space=pltpu.SMEM)
    shape = jax.ShapeDtypeStruct
    dma = pltpu.SemaphoreType.DMA

    def by_block(x):
        return x.reshape(blocks, BSIZE)

    phase, weight, resid, offset = map(by_block, (scan_phase, huber_weight, residual, knot_offset))
    parts, owner_of = pl.pallas_call(
        functools.partial(assemble_kernel, owners, capacity),
        out_shape=(shape((2, chips, PACKED, LANES), f32), shape((blocks + capacity,), jnp.int32)),
        in_specs=[scalars] + [spec] * 5,
        out_specs=(spec, scalars),
        scratch_shapes=[VMEM((GROUP * 64, LANES), f32), VMEM((owners, LANES, LANES), f32)],
        name="assemble",
    )(send_counts.reshape(1, owners), attitude_partials, phase, weight, resid, offset)
    steps = pl.pallas_call(
        functools.partial(exchange_kernel, owners),
        out_shape=shape((owners, 4, LANES), f32),
        in_specs=[spec],
        out_specs=spec,
        scratch_shapes=[VMEM((chips, PACKED, LANES), f32)] * 3
        + [VMEM((owners, 4, LANES), f32)]
        + [dma((chips,))] * 4
        + [dma((owners,))] * 2,
        compiler_params=pltpu.CompilerParams(collective_id=0, has_side_effects=True),
        name="exchange",
    )(parts)
    updated, calsum, srcsum = pl.pallas_call(
        functools.partial(correct_kernel, owners),
        out_shape=(shape((blocks, BSIZE), f32), shape((4, LANES), f32), shape((16, LANES), f32)),
        in_specs=[scalars] + [spec] * 10,
        out_specs=(spec, spec, spec),
        scratch_shapes=[
            VMEM((GROUP * 24, LANES), f32), VMEM((owners, 32, LANES), bf16),
            VMEM((48, 2 * LANES), f32),
        ],
        name="correct",
    )(
        owner_of, steps, attitude_partials, phase, weight, resid, offset,
        by_block(detector_index), calibration_partials, by_block(source_index), source_partials,
    )
    calib, source = pl.pallas_call(
        functools.partial(sums_kernel, owners, segments),
        out_shape=(shape((CALP, CCDS), f32), shape((SP, LANES), f32)),
        in_specs=[spec] * 2,
        out_specs=(spec, spec),
        scratch_shapes=[
            VMEM((owners, 4, LANES), f32), VMEM((segments, 16, LANES), f32),
            dma((owners,)), dma((owners,)), dma((segments,)), dma((segments,)),
        ],
        compiler_params=pltpu.CompilerParams(collective_id=1, has_side_effects=True),
        name="sums",
    )(calsum, srcsum)
    mine = lax.dynamic_index_in_dim(steps, lax.axis_index("src"), 0, keepdims=True)
    return (mine, calib[None], source, updated.reshape(1, blocks * BSIZE))


def solution(mesh):
    return jax.shard_map(
        body,
        mesh=mesh,
        in_specs=(
            P("seg", None, "src"),
            P("seg", "src"),
            P("seg", "src"),
            P("seg", "src"),
            P("seg", "src"),
            P("seg", "src"),
            P("seg", None, "src"),
            P("seg", "src"),
            P("seg", None, "src"),
            P("seg", "src", None),
        ),
        out_specs=(P("seg", None, "src"), P("seg", None, None), P(None, "src"), P("seg", "src")),
        check_vma=False,
    )
```

time: 414 us -> 64.1 us (0.15); the launches traced: 409 us -> 63.8 us
  local copies, waits for them, and re-layouts: 166 us -> 2.44 us
  blocking collectives: 82.7 us -> 0 us
  Pallas kernels: 0 us -> 60.7 us
  other arithmetic: 57.7 us -> 0 us
  matrix products: 38.8 us -> 0 us
  waiting for transfers between devices: 23.6 us -> 0 us
  starting transfers between devices: 19.9 us -> 0 us
  between operations: 15.8 us -> 0.68 us
  loops' own time: 4.5 us -> 0 us
    gather x210 -> x0, local copies, waits for them, and re-layouts: 95.6 us -> none
    psum x2 -> x0, blocking collectives: 82.7 us -> none  [the longest x1 66.2 us: body(): calib_summed = lax.psum(calib_totals, 'src')]
    pallas_call x0 -> x4, Pallas kernels: none -> 60.7 us  [the longest x1 25.9 us: body(): pl.pallas_call(functools.partial(exchange_kernel, owners), out_shape=shap...]
    dot_general x24 -> x0, matrix products: 38.8 us -> none  [the longest x4 17.5 us: add_senders(): jnp.dot(features, knot_hot(group_knots, KN_DEV), precision=highest)]
    mul x48 -> x0, other arithmetic: 37.4 us -> none  [the longest x16 11.6 us: add_sums(): group_weight * group_updated * group_calib]
    all_to_all x3 -> x0, waiting for transfers between devices: 23.6 us -> none  [the longest x1 16 us: body(): lax.all_to_all(outgoing, 'src', split_axis=1, concat_axis=1, tiled=True)]
    mul x12 -> x0, local copies, waits for them, and re-layouts: 21.9 us -> none  [the longest x4 13 us: row_features(): (weight * basis_pairs)[:, None, :] * outer_partials[None]]
    while x52 -> x0, local copies, waits for them, and re-layouts: 20.9 us -> none
  transfers between devices with their start and end apart: 3 -> 0, of which waited for: 2 -> 0; matrix products, arithmetic and copies ran while one was open for 12% -> 0% of each run, Pallas kernels for 0% -> 0%
where the time goes in v1:
time: 64.1 us; the launch traced here: 63.8 us
  Pallas kernels  60.7 us (95%)
  local copies, waits for them, and re-layouts  2.44 us (4%)
  between operations  0.68 us (1%)
    pallas_call x1, Pallas kernels, body(): pl.pallas_call(functools.partial(exchange_kernel, owners), out_shape=shap...  25.9 us
    pallas_call x1, Pallas kernels, body(): pl.pallas_call(functools.partial(sums_kernel, owners, segments), out_shap...  13.8 us
    pallas_call x1, Pallas kernels, body(): pl.pallas_call(functools.partial(correct_kernel, owners), out_shape=(shap...  10.6 us
    pallas_call x1, Pallas kernels, body(): pl.pallas_call(functools.partial(assemble_kernel, owners, capacity), out_...  10.4 us

profile of v1, /device:TPU:1, one launch (start us, length us, event | category | flops | bytes accessed | tf_op | source)
XLA Modules:
  0.0 63.8 jit_solution(1163239832341622568)
XLA Ops:
  0.6 10.4 %assemble.1 = (f32[2,16,48,128]{3,2,1,0:T(8,128)}, s32[136]{0:T(256)}) custom-call(s32[1,32]{1,0:T(1,128)} %bitcast.20, bf16[1,4,16384]{2,1,0:T(4,128)(2,1)} %part_ref.3, f32[128,128]{1,0:T(8,128)} %bitcast.9, f32[128,128]{1,0:T(8,128)} %bitcast.11, f32[128,128]{1,0:T(8,128)} %bitcast.13, s32[128,128]{1,0:T(8,128)} %bitcast.15), custom_call_target="tpu_custom_call" | custom-call | tf_op jit(solution)/shard_map/assemble/pallas_call | solution.py:459
  11.0 25.9 %exchange.1.steps_ref = f32[32,4,128]{2,1,0:T(4,128)} custom-call(f32[2,16,48,128]{3,2,1,0:T(8,128)} %get-tuple-element.11.parts_ref), custom_call_target="tpu_custom_call" | custom-call | tf_op jit(solution)/shard_map/exchange/pallas_call | solution.py:467
  36.9 10.6 %correct.1 = (f32[128,128]{1,0:T(8,128)}, f32[4,128]{1,0:T(4,128)}, f32[16,128]{1,0:T(8,128)}) custom-call(s32[136]{0:T(256)} %get-tuple-element.12.owner_ref, f32[32,4,128]{2,1,0:T(4,128)} %exchange.1.steps_ref, bf16[1,4,16384]{2,1,0:T(4,128)(2,1)} %part_ref.3, f32[128,128]{1,0:T(8,128)} %bitcast.10, f32[128,128]{1,0:T(8,128)} %bitcast.12, ...), custom_call_target="tpu_custom_call" | custom-call | tf_op jit(solution)/shard_map/correct/pallas_call | solution.py:479
  47.6 13.8 %sums.1 = (f32[4,62]{1,0:T(4,128)}, f32[5,128]{1,0:T(8,128)}) custom-call(f32[4,128]{1,0:T(4,128)} %get-tuple-element.13.calsum_ref, f32[16,128]{1,0:T(8,128)} %get-tuple-element.14.srcsum_ref), custom_call_target="tpu_custom_call" | custom-call | tf_op jit(solution)/shard_map/sums/pallas_call | solution.py:493
  61.4 0.0 copy-start.1
  61.4 0.0 copy-start
  61.4 1.3 %constant_dynamic-slice_fusion = f32[1,4,128]{2,1,0:T(4,128)} fusion(f32[32,4,128]{2,1,0:T(4,128)} %exchange.1.steps_ref, s32[]{:T(128)S(6)} %select_n.4), kind=kLoop, calls=%fused_computation | loop fusion | bytes 4100 | tf_op jit(solution)/shard_map/jit(dynamic_index_in_dim)/dynamic_slice | solution.py:505
  62.7 0.0 copy-done.1
  62.7 0.6 copy.16
  63.2 0.0 copy-done
  63.3 0.6 copy.17
Async XLA Ops:
  61.4 1.3 %copy-start.1 = (f32[4,62]{1,0:T(4,128)S(1)}, f32[4,62]{1,0:T(4,128)}, u32[]{:S(2)}) copy-start(f32[4,62]{1,0:T(4,128)} %get-tuple-element.15) | copy-start | bytes 2980
  61.4 1.9 %copy-start = (f32[5,128]{1,0:T(8,128)S(1)}, f32[5,128]{1,0:T(8,128)}, u32[]{:S(2)}) copy-start(f32[5,128]{1,0:T(8,128)} %get-tuple-element.24) | copy-start | bytes 7684

commit v2 on v1

--- a/solution.py
+++ b/solution.py
@@ -209,24 +209,37 @@
     lax.fori_loop(lower, upper, run, 0)
 
 
-def exchange_kernel(
-    owners, parts_ref, out_ref, got_pair, mine, got_chip, got_step,
+def refine_kernel(
+    owners, segments, owner_ref, parts_ref, part_ref, phase_ref, weight_ref, resid_ref,
+    offset_ref, detector_ref, calib_in_ref, source_in_ref, sterm_ref,
+    step_ref, calib_ref, source_ref, updated_ref,
+    got_pair, mine, got_chip, got_step, rows_ref, table_ref, acc_ref,
+    calsum_ref, srcsum_ref, got_cal, got_src,
     pair_send, pair_recv, chip_send, chip_recv, step_send, step_recv,
+    cal_send, cal_recv, src_send, src_recv,
 ):
     chips = owners // 2
     me = lax.axis_index("src")
+    segment = lax.axis_index("seg")
     core = lax.rem(me, 2)
     chip = me // 2
     partner = me + 1 - 2 * core
     barrier = pltpu.get_barrier_semaphore()
 
-    def greet(k):
+    def greet_src(k):
         pl.semaphore_signal(
             barrier, inc=1, device_id={"src": lax.rem(me + k, owners)}, device_id_type=MESH
         )
 
-    loop(1, owners, greet)
-    pl.semaphore_wait(barrier, owners - 1)
+    def greet_seg(k):
+        pl.semaphore_signal(
+            barrier, inc=1, device_id={"seg": lax.rem(segment + k, segments)}, device_id_type=MESH
+        )
+
+    loop(1, owners, greet_src)
+    loop(1, segments, greet_seg)
+    acc_ref[...] = jnp.zeros_like(acc_ref)
+    pl.semaphore_wait(barrier, owners + segments - 2)
 
     def pair_copy(k):
         target_chip = lax.rem(chip + k, chips)
@@ -267,6 +280,7 @@
     total = lax.fori_loop(1, chips, gather, mine[0])
     step = solve_owner([total[8 * t : 8 * t + 8] for t in range(PACKED // 8)])
     got_step[me] = step[0:4]
+    step_ref[0] = step[0:4]
 
     def step_copy(k, slot):
         return pltpu.make_async_remote_copy(
@@ -277,29 +291,13 @@
 
     loop(1, owners, lambda k: step_copy(k, me).start())
 
-    def drain(k):
-        pair_copy(k).wait_send()
-        chip_copy(k).wait_send()
-
-    loop(1, chips, drain)
-    pair_copy(0).wait_send()
-    loop(1, owners, lambda k: step_copy(k, lax.rem(me + k, owners)).wait_recv())
-    out_ref[...] = got_step[...]
-    loop(1, owners, lambda k: step_copy(k, me).wait_send())
-
-
-def correct_kernel(
-    owners, owner_ref, steps_ref, part_ref, phase_ref, weight_ref, resid_ref, offset_ref,
-    detector_ref, calib_ref, source_ref, sterm_ref,
-    updated_ref, calsum_ref, srcsum_ref, rows_ref, table_ref, acc_ref,
-):
     blocks = phase_ref.shape[0]
     stride = 24
     rows = row_ids()
     low = rows < 4
 
-    def make_table(o, carry):
-        x8 = twice(steps_ref[o])
+    def make_table(slot):
+        x8 = twice(got_step[slot])
         table = jnp.concatenate(
             [
                 jnp.where(low, x8, pltpu.roll(x8, LANES - 1, 1)),
@@ -308,11 +306,16 @@
             axis=0,
         )
         high, rest = split_two(table)
-        table_ref[o] = jnp.concatenate([high, rest], axis=0)
-        return carry
-
-    lax.fori_loop(0, owners, make_table, 0)
-    acc_ref[...] = jnp.zeros_like(acc_ref)
+        table_ref[slot] = jnp.concatenate([high, rest], axis=0)
+
+    make_table(me)
+
+    def arrive(k):
+        slot = lax.rem(me + k, owners)
+        step_copy(k, slot).wait_recv()
+        make_table(slot)
+
+    loop(1, owners, arrive)
 
     def group_step(group, carry):
         base = pl.multiple_of(group * GROUP, GROUP)
@@ -323,7 +326,7 @@
             rows_ref[pl.ds(row, GROUP, stride=stride), :] = value
 
         put(0, offset_ref[here, :].astype(f32))
-        put(1, source_ref[here, :].astype(f32))
+        put(1, source_in_ref[here, :].astype(f32))
         put(2, detector_ref[here, :].astype(f32))
         put(3, weight_ref[here, :])
         put(4, resid_ref[here, :])
@@ -350,7 +353,7 @@
             weight = spread(rows_ref, first + 3)
             pull = weight * updated
             sterm = sterm_ref[0, :, lanes].astype(f32)
-            eight = jnp.concatenate([sterm[0:4], calib_ref[0, :, lanes].astype(f32)], axis=0)
+            eight = jnp.concatenate([sterm[0:4], calib_in_ref[0, :, lanes].astype(f32)], axis=0)
             fifth = jnp.broadcast_to(sterm[4:5], (8, LANES))
             last = jnp.where(rows == 0, pull, jnp.where(rows == 1, weight * fifth, 0.0)) * fifth
             high, rest = split_two(
@@ -381,29 +384,6 @@
     lane = lax.broadcasted_iota(jnp.int32, (4, LANES), 1)
     calsum_ref[...] = jnp.where(lane < 64, for_calib[4:8], pltpu.roll(for_calib, 64, 1)[12:16])
 
-
-def sums_kernel(
-    owners, segments, calsum_ref, srcsum_ref, calib_ref, source_ref, got_cal, got_src,
-    cal_send, cal_recv, src_send, src_recv,
-):
-    me = lax.axis_index("src")
-    segment = lax.axis_index("seg")
-    barrier = pltpu.get_barrier_semaphore()
-
-    def greet_src(k):
-        pl.semaphore_signal(
-            barrier, inc=1, device_id={"src": lax.rem(me + k, owners)}, device_id_type=MESH
-        )
-
-    def greet_seg(k):
-        pl.semaphore_signal(
-            barrier, inc=1, device_id={"seg": lax.rem(segment + k, segments)}, device_id_type=MESH
-        )
-
-    loop(1, segments, greet_seg)
-    loop(1, owners, greet_src)
-    pl.semaphore_wait(barrier, owners + segments - 2)
-
     def src_copy(k, slot):
         return pltpu.make_async_remote_copy(
             src_ref=srcsum_ref, dst_ref=got_src.at[slot],
@@ -418,10 +398,18 @@
             device_id={"src": lax.rem(me + k, owners)}, device_id_type=MESH,
         )
 
+    got_src[segment] = srcsum_ref[...]
+    got_cal[me] = calsum_ref[...]
     loop(1, segments, lambda k: src_copy(k, segment).start())
     loop(1, owners, lambda k: cal_copy(k, me).start())
-    got_src[segment] = srcsum_ref[...]
-    got_cal[me] = calsum_ref[...]
+
+    def drain(k):
+        pair_copy(k).wait_send()
+        chip_copy(k).wait_send()
+
+    loop(1, chips, drain)
+    pair_copy(0).wait_send()
+    loop(1, owners, lambda k: step_copy(k, me).wait_send())
     loop(1, segments, lambda k: src_copy(k, lax.rem(segment + k, segments)).wait_recv())
     total = got_src[0]
     for k in range(1, segments):
@@ -433,7 +421,7 @@
     for k in range(1, owners):
         total = total + got_cal[k]
     result = total / (1.0 + pltpu.roll(total, 64, 1))
-    calib_ref[...] = result[:, 0:CCDS]
+    calib_ref[0] = result[:, 0:CCDS]
     loop(1, segments, lambda k: src_copy(k, segment).wait_send())
     loop(1, owners, lambda k: cal_copy(k, me).wait_send())
 
@@ -464,46 +452,31 @@
         scratch_shapes=[VMEM((GROUP * 64, LANES), f32), VMEM((owners, LANES, LANES), f32)],
         name="assemble",
     )(send_counts.reshape(1, owners), attitude_partials, phase, weight, resid, offset)
-    steps = pl.pallas_call(
-        functools.partial(exchange_kernel, owners),
-        out_shape=shape((owners, 4, LANES), f32),
-        in_specs=[spec],
-        out_specs=spec,
+    step, calib, source, updated = pl.pallas_call(
+        functools.partial(refine_kernel, owners, segments),
+        out_shape=(
+            shape((1, 4, LANES), f32), shape((1, CALP, CCDS), f32), shape((SP, LANES), f32),
+            shape((blocks, BSIZE), f32),
+        ),
+        in_specs=[scalars] + [spec] * 10,
+        out_specs=(spec,) * 4,
         scratch_shapes=[VMEM((chips, PACKED, LANES), f32)] * 3
-        + [VMEM((owners, 4, LANES), f32)]
+        + [
+            VMEM((owners, 4, LANES), f32), VMEM((GROUP * 24, LANES), f32),
+            VMEM((owners, 32, LANES), bf16), VMEM((48, 2 * LANES), f32),
+            VMEM((4, LANES), f32), VMEM((16, LANES), f32),
+            VMEM((owners, 4, LANES), f32), VMEM((segments, 16, LANES), f32),
+        ]
         + [dma((chips,))] * 4
-        + [dma((owners,))] * 2,
+        + [dma((owners,))] * 4
+        + [dma((segments,))] * 2,
         compiler_params=pltpu.CompilerParams(collective_id=0, has_side_effects=True),
-        name="exchange",
-    )(parts)
-    updated, calsum, srcsum = pl.pallas_call(
-        functools.partial(correct_kernel, owners),
-        out_shape=(shape((blocks, BSIZE), f32), shape((4, LANES), f32), shape((16, LANES), f32)),
-        in_specs=[scalars] + [spec] * 10,
-        out_specs=(spec, spec, spec),
-        scratch_shapes=[
-            VMEM((GROUP * 24, LANES), f32), VMEM((owners, 32, LANES), bf16),
-            VMEM((48, 2 * LANES), f32),
-        ],
-        name="correct",
+        name="refine",
     )(
-        owner_of, steps, attitude_partials, phase, weight, resid, offset,
+        owner_of, parts, attitude_partials, phase, weight, resid, offset,
         by_block(detector_index), calibration_partials, by_block(source_index), source_partials,
     )
-    calib, source = pl.pallas_call(
-        functools.partial(sums_kernel, owners, segments),
-        out_shape=(shape((CALP, CCDS), f32), shape((SP, LANES), f32)),
-        in_specs=[spec] * 2,
-        out_specs=(spec, spec),
-        scratch_shapes=[
-            VMEM((owners, 4, LANES), f32), VMEM((segments, 16, LANES), f32),
-            dma((owners,)), dma((owners,)), dma((segments,)), dma((segments,)),
-        ],
-        compiler_params=pltpu.CompilerParams(collective_id=1, has_side_effects=True),
-        name="sums",
-    )(calsum, srcsum)
-    mine = lax.dynamic_index_in_dim(steps, lax.axis_index("src"), 0, keepdims=True)
-    return (mine, calib[None], source, updated.reshape(1, blocks * BSIZE))
+    return (step, calib, source, updated.reshape(1, blocks * BSIZE))
 
 
 def solution(mesh):

time: 64.1 us -> 58.2 us (0.908)
  Pallas kernels: 60.7 us -> 53.5 us
  local copies, waits for them, and re-layouts: 2.44 us -> 3.88 us
    pallas_call x3 -> x1, Pallas kernels: 50.4 us -> 43.1 us  [body(): pl.pallas_call(functools.partial(refine_kernel, owners, segments), out_sh...]
    unnamed x6 -> x10, local copies, waits for them, and re-layouts: 1.18 us -> 3.88 us
    dynamic_slice x1 -> x0, local copies, waits for them, and re-layouts: 1.26 us -> none  [body(): lax.dynamic_index_in_dim(steps, lax.axis_index('src'), 0, keepdims=True)]
where the time goes in v2:
time: 58.2 us; the launch traced here: 58 us
  Pallas kernels  53.5 us (92%)
  local copies, waits for them, and re-layouts  3.88 us (7%)
  between operations  0.67 us (1%)
    pallas_call x1, Pallas kernels, body(): pl.pallas_call(functools.partial(refine_kernel, owners, segments), out_sh...  43.1 us
    pallas_call x1, Pallas kernels, body(): pl.pallas_call(functools.partial(assemble_kernel, owners, capacity), out_...  10.4 us
    unnamed x10, local copies, waits for them, and re-layouts  3.88 us

profile of v2, /device:TPU:1, one launch (start us, length us, event | category | flops | bytes accessed | tf_op | source)
XLA Modules:
  0.0 58.0 jit_solution(4115792465030711449)
XLA Ops:
  0.6 10.4 %assemble.1 = (f32[2,16,48,128]{3,2,1,0:T(8,128)}, s32[136]{0:T(256)}) custom-call(s32[1,32]{1,0:T(1,128)} %bitcast.19, bf16[1,4,16384]{2,1,0:T(4,128)(2,1)} %part_ref.3, f32[128,128]{1,0:T(8,128)} %bitcast.8, f32[128,128]{1,0:T(8,128)} %bitcast.10, f32[128,128]{1,0:T(8,128)} %bitcast.12, s32[128,128]{1,0:T(8,128)} %bitcast.14), custom_call_target="tpu_custom_call" | custom-call | tf_op jit(solution)/shard_map/assemble/pallas_call | solution.py:447
  11.0 43.1 %refine.1 = (f32[1,4,128]{2,1,0:T(4,128)}, f32[1,4,62]{2,1,0:T(4,128)}, f32[5,128]{1,0:T(8,128)}, f32[128,128]{1,0:T(8,128)}) custom-call(s32[136]{0:T(256)} %get-tuple-element.10.owner_ref, f32[2,16,48,128]{3,2,1,0:T(8,128)} %get-tuple-element.11.parts_ref, bf16[1,4,16384]{2,1,0:T(4,128)(2,1)} %part_ref.3, f32[128,128]{1,0:T(8,128)} %bitcast.9, ...), custom_call_target="tpu_custom_call" | custom-call | tf_op jit(solution)/shard_map/refine/pallas_call | solution.py:455
  54.2 0.0 copy-start.2
  54.2 0.0 copy-start.1
  54.2 0.6 %copy-done.2 = f32[1,4,128]{2,1,0:T(4,128)S(1)} copy-done((f32[1,4,128]{2,1,0:T(4,128)S(1)}, f32[1,4,128]{2,1,0:T(4,128)}, u32[]{:S(2)}) %copy-start.2) | copy-done | bytes 2072
  54.8 0.0 copy-start
  54.8 0.6 copy.18
  55.4 0.0 copy-done.1
  55.4 0.6 copy.19
  56.0 0.0 copy-done
  56.0 0.6 %copy.20 = f32[5,128]{1,0:T(8,128)} copy(f32[5,128]{1,0:T(8,128)S(1)} %copy-done) | data formatting | bytes 5120
  56.6 1.5 %copy.21 = f32[1,16384]{1,0:T(1,128)} copy(f32[1,16384]{1,0:T(1,128)} %bitcast.18) | data formatting | bytes 131072
Async XLA Ops:
  54.2 0.7 %copy-start.2 = (f32[1,4,128]{2,1,0:T(4,128)S(1)}, f32[1,4,128]{2,1,0:T(4,128)}, u32[]{:S(2)}) copy-start(f32[1,4,128]{2,1,0:T(4,128)} %get-tuple-element.20) | copy-start | bytes 6148
  54.2 1.2 %copy-start.1 = (f32[1,4,62]{2,1,0:T(4,128)S(1)}, f32[1,4,62]{2,1,0:T(4,128)}, u32[]{:S(2)}) copy-start(f32[1,4,62]{2,1,0:T(4,128)} %get-tuple-element.21) | copy-start | bytes 2980
  54.8 1.2 %copy-start = (f32[5,128]{1,0:T(8,128)S(1)}, f32[5,128]{1,0:T(8,128)}, u32[]{:S(2)}) copy-start(f32[5,128]{1,0:T(8,128)} %get-tuple-element.22) | copy-start | bytes 7684

commit v3 on v2

--- a/solution.py
+++ b/solution.py
@@ -213,7 +213,8 @@
     owners, segments, owner_ref, parts_ref, part_ref, phase_ref, weight_ref, resid_ref,
     offset_ref, detector_ref, calib_in_ref, source_in_ref, sterm_ref,
     step_ref, calib_ref, source_ref, updated_ref,
-    got_pair, mine, got_chip, got_step, rows_ref, table_ref, acc_ref,
+    got_pair, mine, got_chip, got_step, rows_ref, table_ref, pull_acc, damp_acc,
+    hot_ref, right_ref, design_ref, scaled_ref,
     calsum_ref, srcsum_ref, got_cal, got_src,
     pair_send, pair_recv, chip_send, chip_recv, step_send, step_recv,
     cal_send, cal_recv, src_send, src_recv,
@@ -238,7 +239,57 @@
 
     loop(1, owners, greet_src)
     loop(1, segments, greet_seg)
-    acc_ref[...] = jnp.zeros_like(acc_ref)
+    blocks = phase_ref.shape[0]
+    groups = blocks // GROUP
+    stride = 24
+    rows = row_ids()
+    low = rows < 4
+    pull_acc[...] = jnp.zeros_like(pull_acc)
+    damp_acc[...] = jnp.zeros_like(damp_acc)
+
+    def prepare(group):
+        base = pl.multiple_of(group * GROUP, GROUP)
+        here = pl.ds(base, GROUP)
+        spline = spline_basis(phase_ref[here, :])
+
+        def put(row, value):
+            rows_ref[pl.ds(row, GROUP, stride=stride), :] = value
+
+        put(0, offset_ref[here, :].astype(f32))
+        put(1, source_in_ref[here, :].astype(f32))
+        put(2, detector_ref[here, :].astype(f32))
+        put(3, weight_ref[here, :])
+        for i in range(4):
+            for j in range(4):
+                put(8 + 4 * i + j, spline[i])
+        lefts = []
+        for q in range(GROUP):
+            first = q * stride
+            lanes = pl.ds(pl.multiple_of((base + q) * BSIZE, BSIZE), BSIZE)
+            here_lanes = slice(q * BSIZE, (q + 1) * BSIZE)
+            a8 = twice(part_ref[0, :, lanes].astype(f32))
+            design_ref[base + q, 0:8] = a8 * rows_ref[pl.ds(first + 8, 8), :]
+            design_ref[base + q, 8:16] = a8 * rows_ref[pl.ds(first + 16, 8), :]
+            hot_ref[base + q] = one_hot(rows_ref[pl.ds(first, 1), :], LANES)
+            right_ref[group, 0:LANES, here_lanes] = one_hot(rows_ref[pl.ds(first + 1, 1), :], LANES)
+            right_ref[group, LANES:, here_lanes] = one_hot(rows_ref[pl.ds(first + 2, 1), :], LANES)
+            weight = spread(rows_ref, first + 3)
+            sterm = sterm_ref[0, :, lanes].astype(f32)
+            eight = jnp.concatenate([sterm[0:4], calib_in_ref[0, :, lanes].astype(f32)], axis=0)
+            fifth = jnp.broadcast_to(sterm[4:5], (8, LANES))
+            scaled = weight * eight
+            scaled_fifth = jnp.where(rows == 0, weight * fifth, 0.0)
+            scaled_ref[base + q, 0:8] = scaled
+            scaled_ref[base + q, 8:16] = scaled_fifth
+            high, rest = split_two(jnp.concatenate([scaled * eight, scaled_fifth * fifth], axis=0))
+            lefts.append(jnp.concatenate([high, rest], axis=0))
+        damp_acc[...] += lax.dot_general(
+            jnp.concatenate(lefts, axis=1), right_ref[group], nt, preferred_element_type=f32
+        )
+
+    early = groups // 4
+    middle = 3 * groups // 4
+    loop(0, early, prepare)
     pl.semaphore_wait(barrier, owners + segments - 2)
 
     def pair_copy(k):
@@ -272,6 +323,7 @@
     loop(2, chips, add_and_send)
     add_pair(0)
     chip_copy(chips - 1).start()
+    loop(early, middle, prepare)
 
     def gather(k, total):
         chip_copy(k).wait_recv()
@@ -290,11 +342,7 @@
         )
 
     loop(1, owners, lambda k: step_copy(k, me).start())
-
-    blocks = phase_ref.shape[0]
-    stride = 24
-    rows = row_ids()
-    low = rows < 4
+    loop(middle, groups, prepare)
 
     def make_table(slot):
         x8 = twice(got_step[slot])
@@ -317,72 +365,40 @@
 
     loop(1, owners, arrive)
 
-    def group_step(group, carry):
+    def correct(group):
         base = pl.multiple_of(group * GROUP, GROUP)
-        here = pl.ds(base, GROUP)
-        spline = spline_basis(phase_ref[here, :])
-
-        def put(row, value):
-            rows_ref[pl.ds(row, GROUP, stride=stride), :] = value
-
-        put(0, offset_ref[here, :].astype(f32))
-        put(1, source_in_ref[here, :].astype(f32))
-        put(2, detector_ref[here, :].astype(f32))
-        put(3, weight_ref[here, :])
-        put(4, resid_ref[here, :])
-        for i in range(4):
-            for j in range(4):
-                put(8 + 4 * i + j, spline[i])
         lefts = []
-        rights = []
         for q in range(GROUP):
-            first = q * stride
-            lanes = pl.ds(pl.multiple_of((base + q) * BSIZE, BSIZE), BSIZE)
-            a8 = twice(part_ref[0, :, lanes].astype(f32))
-            hot = one_hot(rows_ref[pl.ds(first, 1), :], LANES)
-            values = jnp.dot(table_ref[owner_ref[base + q]], hot, preferred_element_type=f32)
-            term = a8 * (
-                rows_ref[pl.ds(first + 8, 8), :] * (values[0:8] + values[16:24])
-                + rows_ref[pl.ds(first + 16, 8), :] * (values[8:16] + values[24:32])
+            block = base + q
+            values = jnp.dot(
+                table_ref[owner_ref[block]], hot_ref[block], preferred_element_type=f32
             )
+            term = design_ref[block, 0:8] * (values[0:8] + values[16:24]) + design_ref[
+                block, 8:16
+            ] * (values[8:16] + values[24:32])
             term = term + pltpu.roll(term, 4, 0)
             term = term + pltpu.roll(term, 2, 0)
             term = term + pltpu.roll(term, 1, 0)
-            updated = spread(rows_ref, first + 4) - term
-            updated_ref[pl.ds(base + q, 1), :] = updated[0:1]
-            weight = spread(rows_ref, first + 3)
-            pull = weight * updated
-            sterm = sterm_ref[0, :, lanes].astype(f32)
-            eight = jnp.concatenate([sterm[0:4], calib_in_ref[0, :, lanes].astype(f32)], axis=0)
-            fifth = jnp.broadcast_to(sterm[4:5], (8, LANES))
-            last = jnp.where(rows == 0, pull, jnp.where(rows == 1, weight * fifth, 0.0)) * fifth
+            updated = spread(resid_ref, block) - term
+            updated_ref[pl.ds(block, 1), :] = updated[0:1]
             high, rest = split_two(
-                jnp.concatenate([pull * eight, weight * eight * eight, last], axis=0)
-            )
-            lefts.append(jnp.concatenate([high.astype(f32), rest.astype(f32)], axis=0).astype(bf16))
-            rights.append(
                 jnp.concatenate(
-                    [
-                        one_hot(rows_ref[pl.ds(first + 1, 1), :], LANES),
-                        one_hot(rows_ref[pl.ds(first + 2, 1), :], LANES),
-                    ],
-                    axis=0,
+                    [updated * scaled_ref[block, 0:8], updated * scaled_ref[block, 8:16]], axis=0
                 )
             )
-        acc_ref[...] += lax.dot_general(
-            jnp.concatenate(lefts, axis=1), jnp.concatenate(rights, axis=1), nt,
-            preferred_element_type=f32,
-        )
-        return carry
-
-    lax.fori_loop(0, blocks // GROUP, group_step, 0)
-    sums = acc_ref[0:24] + acc_ref[24:48]
-    for_source = sums[:, 0:LANES]
-    for_calib = sums[:, LANES : 2 * LANES]
-    srcsum_ref[0:8] = jnp.concatenate([for_source[0:4], for_source[8:12]], axis=0)
-    srcsum_ref[8:16] = for_source[16:24]
-    lane = lax.broadcasted_iota(jnp.int32, (4, LANES), 1)
-    calsum_ref[...] = jnp.where(lane < 64, for_calib[4:8], pltpu.roll(for_calib, 64, 1)[12:16])
+            lefts.append(jnp.concatenate([high, rest], axis=0))
+        pull_acc[...] += lax.dot_general(
+            jnp.concatenate(lefts, axis=1), right_ref[group], nt, preferred_element_type=f32
+        )
+
+    loop(0, groups, correct)
+    pull = pull_acc[0:16] + pull_acc[16:32]
+    damp = damp_acc[0:16] + damp_acc[16:32]
+    srcsum_ref[0:8] = jnp.concatenate([pull[0:4, 0:LANES], damp[0:4, 0:LANES]], axis=0)
+    srcsum_ref[8:16] = pull[8:16, 0:LANES] + pltpu.roll(damp[8:16, 0:LANES], 1, 0)
+    lane = lax.broadcasted_iota(jnp.int32, (8, LANES), 1)
+    both = jnp.where(lane < 64, pull[0:8, LANES:], pltpu.roll(damp[0:8, LANES:], 64, 1))
+    calsum_ref[...] = both[4:8]
 
     def src_copy(k, slot):
         return pltpu.make_async_remote_copy(
@@ -426,6 +442,11 @@
     loop(1, owners, lambda k: cal_copy(k, me).wait_send())
 
 
+def hand_out_kernel(*refs):
+    for given, out in zip(refs[:4], refs[4:]):
+        out[...] = given[...]
+
+
 def body(
     attitude_partials, scan_phase, huber_weight, residual, knot_offset, detector_index,
     calibration_partials, source_index, source_partials, send_counts,
@@ -452,30 +473,43 @@
         scratch_shapes=[VMEM((GROUP * 64, LANES), f32), VMEM((owners, LANES, LANES), f32)],
         name="assemble",
     )(send_counts.reshape(1, owners), attitude_partials, phase, weight, resid, offset)
-    step, calib, source, updated = pl.pallas_call(
+    results = (
+        shape((1, 4, LANES), f32), shape((1, CALP, CCDS), f32), shape((SP, LANES), f32),
+        shape((blocks, BSIZE), f32),
+    )
+    refined = pl.pallas_call(
         functools.partial(refine_kernel, owners, segments),
-        out_shape=(
-            shape((1, 4, LANES), f32), shape((1, CALP, CCDS), f32), shape((SP, LANES), f32),
-            shape((blocks, BSIZE), f32),
-        ),
+        out_shape=results,
         in_specs=[scalars] + [spec] * 10,
         out_specs=(spec,) * 4,
         scratch_shapes=[VMEM((chips, PACKED, LANES), f32)] * 3
         + [
             VMEM((owners, 4, LANES), f32), VMEM((GROUP * 24, LANES), f32),
-            VMEM((owners, 32, LANES), bf16), VMEM((48, 2 * LANES), f32),
+            VMEM((owners, 32, LANES), bf16), VMEM((32, 2 * LANES), f32),
+            VMEM((32, 2 * LANES), f32), VMEM((blocks, LANES, BSIZE), bf16),
+            VMEM((blocks // GROUP, 2 * LANES, GROUP * BSIZE), bf16),
+            VMEM((blocks, 16, BSIZE), f32), VMEM((blocks, 16, BSIZE), f32),
             VMEM((4, LANES), f32), VMEM((16, LANES), f32),
             VMEM((owners, 4, LANES), f32), VMEM((segments, 16, LANES), f32),
         ]
         + [dma((chips,))] * 4
         + [dma((owners,))] * 4
         + [dma((segments,))] * 2,
-        compiler_params=pltpu.CompilerParams(collective_id=0, has_side_effects=True),
+        compiler_params=pltpu.CompilerParams(
+            collective_id=0, has_side_effects=True, vmem_limit_bytes=67043328
+        ),
         name="refine",
     )(
         owner_of, parts, attitude_partials, phase, weight, resid, offset,
         by_block(detector_index), calibration_partials, by_block(source_index), source_partials,
     )
+    step, calib, source, updated = pl.pallas_call(
+        hand_out_kernel,
+        out_shape=results,
+        in_specs=[spec] * 4,
+        out_specs=(spec,) * 4,
+        name="hand_out",
+    )(*refined)
     return (step, calib, source, updated.reshape(1, blocks * BSIZE))
 
 

time: 58.2 us -> 55.5 us (0.954)
  local copies, waits for them, and re-layouts: 3.88 us -> 0 us
  Pallas kernels: 53.5 us -> 54.7 us
    unnamed x10 -> x0, local copies, waits for them, and re-layouts: 3.88 us -> none
    pallas_call x0 -> x1, Pallas kernels: none -> 1.5 us  [body(): pl.pallas_call(hand_out_kernel, out_shape=results, in_specs=[spec] * 4, o...]
where the time goes in v3:
time: 55.5 us; the launch traced here: 55.3 us
  Pallas kernels  54.7 us (99%)
  between operations  0.65 us (1%)
    pallas_call x1, Pallas kernels, body(): pl.pallas_call(functools.partial(refine_kernel, owners, segments), out_sh...  42.8 us
    pallas_call x1, Pallas kernels, body(): pl.pallas_call(functools.partial(assemble_kernel, owners, capacity), out_...  10.4 us
    pallas_call x1, Pallas kernels, body(): pl.pallas_call(hand_out_kernel, out_shape=results, in_specs=[spec] * 4, o...  1.5 us

profile of v3, /device:TPU:1, one launch (start us, length us, event | category | flops | bytes accessed | tf_op | source)
XLA Modules:
  0.0 55.3 jit_solution(7444912475917324432)
XLA Ops:
  0.6 10.4 %assemble.1 = (f32[2,16,48,128]{3,2,1,0:T(8,128)}, s32[136]{0:T(256)}) custom-call(s32[1,32]{1,0:T(1,128)} %bitcast.18, bf16[1,4,16384]{2,1,0:T(4,128)(2,1)} %part_ref.3, f32[128,128]{1,0:T(8,128)} %bitcast.8, f32[128,128]{1,0:T(8,128)} %bitcast.10, f32[128,128]{1,0:T(8,128)} %bitcast.12, s32[128,128]{1,0:T(8,128)} %bitcast.14), custom_call_target="tpu_custom_call" | custom-call | tf_op jit(solution)/shard_map/assemble/pallas_call | solution.py:468
  11.0 42.8 %refine.1 = (f32[1,4,128]{2,1,0:T(4,128)}, f32[1,4,62]{2,1,0:T(4,128)}, f32[5,128]{1,0:T(8,128)}, f32[128,128]{1,0:T(8,128)}) custom-call(s32[136]{0:T(256)} %get-tuple-element.14.owner_ref, f32[2,16,48,128]{3,2,1,0:T(8,128)} %get-tuple-element.15.parts_ref, bf16[1,4,16384]{2,1,0:T(4,128)(2,1)} %part_ref.3, f32[128,128]{1,0:T(8,128)} %bitcast.9, ...), custom_call_target="tpu_custom_call" | custom-call | tf_op jit(solution)/shard_map/refine/pallas_call | solution.py:480
  53.8 1.5 %hand_out.1 = (f32[1,4,128]{2,1,0:T(4,128)}, f32[1,4,62]{2,1,0:T(4,128)}, f32[5,128]{1,0:T(8,128)}, f32[128,128]{1,0:T(8,128)}) custom-call(f32[1,4,128]{2,1,0:T(4,128)} %get-tuple-element.16.refs_0_, f32[1,4,62]{2,1,0:T(4,128)} %get-tuple-element.17.refs_1_, f32[5,128]{1,0:T(8,128)} %get-tuple-element.18.refs_2_, f32[128,128]{1,0:T(8,128)} %get-tuple-element.19.refs_3_), custom_call_target="tpu_custom_call" | custom-call | tf_op jit(solution)/shard_map/hand_out/pallas_call | solution.py:506

commit v4 on v3

--- a/solution.py
+++ b/solution.py
@@ -271,8 +271,8 @@
             design_ref[base + q, 0:8] = a8 * rows_ref[pl.ds(first + 8, 8), :]
             design_ref[base + q, 8:16] = a8 * rows_ref[pl.ds(first + 16, 8), :]
             hot_ref[base + q] = one_hot(rows_ref[pl.ds(first, 1), :], LANES)
-            right_ref[group, 0:LANES, here_lanes] = one_hot(rows_ref[pl.ds(first + 1, 1), :], LANES)
-            right_ref[group, LANES:, here_lanes] = one_hot(rows_ref[pl.ds(first + 2, 1), :], LANES)
+            right_ref[group, here_lanes, 0:LANES] = one_hot(rows_ref[pl.ds(first + 1, 1), :], LANES).T
+            right_ref[group, here_lanes, LANES:] = one_hot(rows_ref[pl.ds(first + 2, 1), :], LANES).T
             weight = spread(rows_ref, first + 3)
             sterm = sterm_ref[0, :, lanes].astype(f32)
             eight = jnp.concatenate([sterm[0:4], calib_in_ref[0, :, lanes].astype(f32)], axis=0)
@@ -283,8 +283,8 @@
             scaled_ref[base + q, 8:16] = scaled_fifth
             high, rest = split_two(jnp.concatenate([scaled * eight, scaled_fifth * fifth], axis=0))
             lefts.append(jnp.concatenate([high, rest], axis=0))
-        damp_acc[...] += lax.dot_general(
-            jnp.concatenate(lefts, axis=1), right_ref[group], nt, preferred_element_type=f32
+        damp_acc[...] += jnp.dot(
+            jnp.concatenate(lefts, axis=1), right_ref[group], preferred_element_type=f32
         )
 
     early = groups // 4
@@ -387,8 +387,8 @@
                 )
             )
             lefts.append(jnp.concatenate([high, rest], axis=0))
-        pull_acc[...] += lax.dot_general(
-            jnp.concatenate(lefts, axis=1), right_ref[group], nt, preferred_element_type=f32
+        pull_acc[...] += jnp.dot(
+            jnp.concatenate(lefts, axis=1), right_ref[group], preferred_element_type=f32
         )
 
     loop(0, groups, correct)
@@ -487,7 +487,7 @@
             VMEM((owners, 4, LANES), f32), VMEM((GROUP * 24, LANES), f32),
             VMEM((owners, 32, LANES), bf16), VMEM((32, 2 * LANES), f32),
             VMEM((32, 2 * LANES), f32), VMEM((blocks, LANES, BSIZE), bf16),
-            VMEM((blocks // GROUP, 2 * LANES, GROUP * BSIZE), bf16),
+            VMEM((blocks // GROUP, GROUP * BSIZE, 2 * LANES), bf16),
             VMEM((blocks, 16, BSIZE), f32), VMEM((blocks, 16, BSIZE), f32),
             VMEM((4, LANES), f32), VMEM((16, LANES), f32),
             VMEM((owners, 4, LANES), f32), VMEM((segments, 16, LANES), f32),

time: 55.5 us -> 55.2 us (level)
  no operation moved by 1% of the time
where the time goes in v4:
time: 55.2 us; the launch traced here: 55 us
  Pallas kernels  54.4 us (99%)
  between operations  0.65 us (1%)
    pallas_call x1, Pallas kernels, body(): pl.pallas_call(functools.partial(refine_kernel, owners, segments), out_sh...  42.5 us
    pallas_call x1, Pallas kernels, body(): pl.pallas_call(functools.partial(assemble_kernel, owners, capacity), out_...  10.4 us
    pallas_call x1, Pallas kernels, body(): pl.pallas_call(hand_out_kernel, out_shape=results, in_specs=[spec] * 4, o...  1.5 us

profile of v4, /device:TPU:1, one launch (start us, length us, event | category | flops | bytes accessed | tf_op | source)
XLA Modules:
  0.0 55.0 jit_solution(17714912791960525667)
XLA Ops:
  0.6 10.4 %assemble.1 = (f32[2,16,48,128]{3,2,1,0:T(8,128)}, s32[136]{0:T(256)}) custom-call(s32[1,32]{1,0:T(1,128)} %bitcast.18, bf16[1,4,16384]{2,1,0:T(4,128)(2,1)} %part_ref.3, f32[128,128]{1,0:T(8,128)} %bitcast.8, f32[128,128]{1,0:T(8,128)} %bitcast.10, f32[128,128]{1,0:T(8,128)} %bitcast.12, s32[128,128]{1,0:T(8,128)} %bitcast.14), custom_call_target="tpu_custom_call" | custom-call | tf_op jit(solution)/shard_map/assemble/pallas_call | solution.py:468
  11.0 42.5 %refine.1 = (f32[1,4,128]{2,1,0:T(4,128)}, f32[1,4,62]{2,1,0:T(4,128)}, f32[5,128]{1,0:T(8,128)}, f32[128,128]{1,0:T(8,128)}) custom-call(s32[136]{0:T(256)} %get-tuple-element.14.owner_ref, f32[2,16,48,128]{3,2,1,0:T(8,128)} %get-tuple-element.15.parts_ref, bf16[1,4,16384]{2,1,0:T(4,128)(2,1)} %part_ref.3, f32[128,128]{1,0:T(8,128)} %bitcast.9, ...), custom_call_target="tpu_custom_call" | custom-call | tf_op jit(solution)/shard_map/refine/pallas_call | solution.py:480
  53.5 1.5 %hand_out.1 = (f32[1,4,128]{2,1,0:T(4,128)}, f32[1,4,62]{2,1,0:T(4,128)}, f32[5,128]{1,0:T(8,128)}, f32[128,128]{1,0:T(8,128)}) custom-call(f32[1,4,128]{2,1,0:T(4,128)} %get-tuple-element.16.refs_0_, f32[1,4,62]{2,1,0:T(4,128)} %get-tuple-element.17.refs_1_, f32[5,128]{1,0:T(8,128)} %get-tuple-element.18.refs_2_, f32[128,128]{1,0:T(8,128)} %get-tuple-element.19.refs_3_), custom_call_target="tpu_custom_call" | custom-call | tf_op jit(solution)/shard_map/hand_out/pallas_call | solution.py:506
